TPU v7x, 128 devices: a whole 4x4x4 slice. The times are simulated.
128 devices in a mesh: row: 32 (over z, x, core), col: 4 (over y).
Axes of the slice: x: 4, y: 4, z: 4, core: 2. Of those that a mesh axis runs over, the one named last changes fastest.
Arguments:
- state: float32 [2, 32768, 4096], P(None, 'row', 'col'), may hold values from -6 to 6
- panel: float32 [2, 32768, 2048], P(None, 'row', 'col'), may hold values from -1 to 1
- pivots: int32 [64], replicated, may hold values from 0 to 63, each once
Outputs:
- adjoint: float32 [2, 32768, 4096], P(None, 'row', 'col')
Inputs may be any that keep to these rules, and one draw needn't show every extreme that they name: pivots names every block index once.
All inputs are finite; a program needn't handle non-finite values.
Results may differ from a plain program's by a relative error of at most 0.00007.
Values sent between devices are 32-bit elements; how exact they have to be, the bound alone decides.
A program may use at most 192 MiB of HBM per device.

v0:
```python
import jax
import jax.numpy as jnp
from jax import lax
from jax.sharding import PartitionSpec as P


def unit_solve(block, right):
    lower = jnp.tril(block, -1) + jnp.eye(block.shape[0], dtype=block.dtype)
    return lax.linalg.triangular_solve(
        lower, right, left_side=True, lower=True, transpose_a=True, unit_diagonal=True
    )


def contract(part, values, weight):
    return jnp.einsum(
        "lic,lir->cr", part, values * weight[:, None, None], precision=lax.Precision.HIGHEST
    )


def finish_panel(term, block, which, position):
    total = lax.psum(term, "row")
    own_block = jnp.where(position == which, block, jnp.zeros_like(block))
    return unit_solve(own_block, total)


def body(state, panel, pivots):
    nrows = lax.axis_size("row")
    position = lax.axis_index("row")
    slots = state.shape[0]
    width = state.shape[1]
    columns = lax.all_gather(panel, "col", axis=2, tiled=True)
    block_ids = jnp.arange(slots) * nrows + position
    from_two = (block_ids >= 2).astype(jnp.float32)
    from_one = (block_ids >= 1).astype(jnp.float32)
    first_slot = state[0]
    zeros_block = jnp.zeros_like(first_slot)
    upper_sum = contract(columns[:, :, width:], state, from_two)
    term_one = jnp.where(position == 1, first_slot, zeros_block) - upper_sum
    solved_one = finish_panel(term_one, columns[0, :, width:], 1, position)
    updated = state.at[0].set(jnp.where(position == 1, solved_one, first_slot))
    lower_sum = contract(columns[:, :, :width], updated, from_one)
    term_zero = jnp.where(position == 0, first_slot, zeros_block) - lower_sum
    solved_zero = finish_panel(term_zero, columns[0, :, :width], 0, position)
    finished = updated.at[0].set(
        jnp.where(position == 1, solved_one, jnp.where(position == 0, solved_zero, updated[0]))
    )
    incoming = lax.all_to_all(finished, "row", split_axis=2, concat_axis=0, tiled=True)
    share_cols = incoming.shape[2]
    total_blocks = incoming.shape[0]
    flat_blocks = incoming.reshape(total_blocks, width * share_cols)
    target = jnp.arange(total_blocks, dtype=jnp.int32)
    target_block = target % slots * nrows + target // slots
    source_block = jnp.take(pivots, target_block, axis=0)
    source_place = source_block % nrows * slots + source_block // nrows
    moved = jnp.take(flat_blocks, source_place, axis=0)
    returning = moved.reshape(total_blocks, width, share_cols)
    return lax.all_to_all(returning, "row", split_axis=0, concat_axis=2, tiled=True)


def solution(mesh):
    placed = (P(None, "row", "col"), P(None, "row", "col"), P())
    return jax.shard_map(
        body, mesh=mesh, in_specs=placed, out_specs=P(None, "row", "col"), check_vma=False
    )
```

profile of v0, /device:TPU:97, one launch (start us, length us, event | category | flops | bytes accessed | tf_op | source)
XLA Modules:
  0.0 871.6 jit_solution(6558359645149398802)
XLA Ops:
  6.5 0.7 all-gather.2.cloned.1.call-update
  7.3 8.4 copy.92
  15.8 148.6 %all-gather.2.cloned.1.call-done = f32[2,1024,2048]{2,1,0:T(8,128)} async-done(((f32[2,1024,512]{2,1,0:T(8,128)}), f32[2,1024,2048]{2,1,0:T(8,128)}) %all-gather.2.cloned.1.call-update) | async-done | bytes 16777232 | tf_op jit(solution)/shard_map/all_gather | solution.py:31
  164.4 34.3 %bitcast_subtract_fusion.1 = f32[1024,1024]{1,0:T(8,128)} fusion(f32[2,1024,1024]{2,1,0:T(8,128)} %param.9, pred[]{:T(512)S(6)} %eq.20, f32[2,1024,2048]{2,1,0:T(8,128)} %all-gather.2.cloned.1.call-done, f32[2]{0:T(128)S(1)} %compare_convert_fusion.1), kind=kOutput, calls=%fused_computation.26 | convolution fusion | flops 25773998080 | bytes 25165832 | tf_op jit(solution)/shard_map/lic,lir->cr/dot_general | solution.py:15
  199.0 6.9 convert_add_fusion
  206.0 23.8 %while.6 = (s32[]{:T(128)}, f32[1024,1024]{1,0:T(8,128)}, s32[8,2]{0,1:T(2,128)S(1)}, f32[8,128,128]{2,1,0:T(8,128)S(1)}, s32[]{:T(128)}) while((s32[]{:T(128)}, f32[1024,1024]{1,0:T(8,128)}, s32[8,2]{0,1:T(2,128)S(1)}, f32[8,128,128]{2,1,0:T(8,128)S(1)}, s32[]{:T(128)}) %tuple.50), condition=%wide.while_cond.2, body=%wide.while_body.2.sunk | while | flops 2 | bytes 131181 | solution.py:9
  206.7 2.3 bitcast_dynamic-update-slice_fusion.6
  209.7 2.3 bitcast_dynamic-update-slice_fusion.6
  212.7 2.3 bitcast_dynamic-update-slice_fusion.6
  215.7 2.3 bitcast_dynamic-update-slice_fusion.6
  218.6 2.3 bitcast_dynamic-update-slice_fusion.6
  221.6 2.3 bitcast_dynamic-update-slice_fusion.6
  224.6 2.3 bitcast_dynamic-update-slice_fusion.6
  227.6 2.2 bitcast_dynamic-update-slice_fusion.6
  229.8 78.6 %custom-call.4 = f32[8,128,128]{1,2,0:T(8,128)S(1)} custom-call(f32[8,128,128]{2,1,0:T(8,128)S(1)} %get-tuple-element.44), custom_call_target="InvertDiagBlocksLowerTriangular" | custom-call | tf_op jit(solution)/shard_map/triangular_solve/custom-call.1 | solution.py:9
  308.4 3.4 all-reduce.3.cloned.1.call-done
  311.8 1.8 fusion.70
  313.6 1.7 convolution_subtract_fusion.9
  315.9 1.8 convolution_subtract_fusion.1
  318.3 2.0 fusion.53
  321.0 2.2 fusion.59
  324.0 2.6 convolution_subtract_fusion.5
  327.5 2.8 convolution_subtract_fusion.3
  331.2 13.3 %convolution_subtract_fusion.8 = f32[128,1024]{1,0:T(8,128)S(1)} fusion(f32[896,1024]{1,0:T(8,128)S(1)} %constant_dynamic-update-slice_fusion.11, f32[1024,1024]{1,0:T(8,128)S(1)} %copy-done.4, f32[1024,1024]{1,0:T(8,128)} %get-tuple-element.174), kind=kOutput, calls=%fused_computation.79 | convolution fusion | flops 1409417216 | bytes 5177344 | tf_op jit(solution)/shard_map/triangular_solve/dot.28 | solution.py:9
  345.5 1.3 slice-done.1
  346.8 0.9 bitcast_select_fusion.1
  347.7 1.3 copy-done.2
  349.0 2.6 bitcast_dynamic-update-slice_fusion.3
  351.6 34.1 %bitcast_subtract_fusion = f32[1024,1024]{1,0:T(8,128)} fusion(f32[2,1024,1024]{2,1,0:T(8,128)S(1)} %bitcast.157, pred[]{:T(512)S(6)} %eq.22, f32[2,1024,2048]{2,1,0:T(8,128)} %all-gather.2.cloned.1.call-done, f32[2,1024,1024]{2,1,0:T(8,128)} %bitcast_dynamic-update-slice_fusion.3, f32[2]{0:T(128)S(1)} %compare_convert_fusion), kind=kOutput, calls=%fused_computation.25 | convolution fusion | flops 25773998080 | bytes 25165832 | tf_op jit(solution)/shard_map/lic,lir->cr/dot_general | solution.py:15
  385.8 22.6 %while.7 = (s32[]{:T(128)}, f32[1024,1024]{1,0:T(8,128)}, s32[8,2]{0,1:T(2,128)S(1)}, f32[8,128,128]{2,1,0:T(8,128)S(1)}, s32[]{:T(128)}) while((s32[]{:T(128)}, f32[1024,1024]{1,0:T(8,128)}, s32[8,2]{0,1:T(2,128)S(1)}, f32[8,128,128]{2,1,0:T(8,128)S(1)}, s32[]{:T(128)}) %tuple.62), condition=%wide.while_cond.2.clone, body=%wide.while_body.2.clone.sunk | while | flops 2 | bytes 131181 | solution.py:9
  386.4 2.2 bitcast_dynamic-update-slice_fusion.7
  389.2 2.2 bitcast_dynamic-update-slice_fusion.7
  392.0 2.2 bitcast_dynamic-update-slice_fusion.7
  394.9 2.2 bitcast_dynamic-update-slice_fusion.7
  397.7 2.2 bitcast_dynamic-update-slice_fusion.7
  400.5 2.2 bitcast_dynamic-update-slice_fusion.7
  403.3 2.2 bitcast_dynamic-update-slice_fusion.7
  406.2 2.1 bitcast_dynamic-update-slice_fusion.7
  408.3 79.0 %custom-call.5 = f32[8,128,128]{1,2,0:T(8,128)S(1)} custom-call(f32[8,128,128]{2,1,0:T(8,128)S(1)} %get-tuple-element.45), custom_call_target="InvertDiagBlocksLowerTriangular" | custom-call | tf_op jit(solution)/shard_map/triangular_solve/custom-call.1 | solution.py:9
  487.3 10.6 %all-reduce.5.cloned.1.call-done = f32[1024,1024]{1,0:T(8,128)} async-done(((f32[1024,1024]{1,0:T(8,128)}), f32[1024,1024]{1,0:T(8,128)}) %all-reduce.5.cloned.1.call-update) | async-done | bytes 4194320 | tf_op jit(solution)/shard_map/psum | solution.py:21
  498.0 1.8 fusion.68
  499.7 1.7 convolution_subtract_fusion.7
  502.0 1.8 convolution_subtract_fusion
  504.5 2.0 fusion.50
  507.1 2.2 fusion.56
  510.1 2.6 convolution_subtract_fusion.4
  513.6 2.8 convolution_subtract_fusion.2
  517.4 3.5 convolution_subtract_fusion.6
  521.9 2.5 slice-done.3
  524.4 3.5 bitcast_dynamic-update-slice_fusion.2
  527.9 13.3 %copy.48 = f32[2,1024,1024]{1,0,2:T(2,128)} copy(f32[2,1024,1024]{2,1,0:T(8,128)} %bitcast_dynamic-update-slice_fusion.2) | data formatting | bytes 16777216 | tf_op jit(solution)/shard_map/scatter | solution.py:44
  541.2 6.6 all-to-all-start
  547.9 0.8 gather_fusion
  548.8 96.3 %all-to-all-done = f32[2,1024,1024]{1,0,2:T(2,128)} async-done(((f32[2,1024,1024]{1,0,2:T(2,128)}), f32[2,1024,1024]{1,0,2:T(2,128)}, u32[]{:S(2)}, u32[]{:S(2)}) %all-to-all-start) | async-done | bytes 8388640 | tf_op jit(solution)/shard_map/all_to_all | solution.py:47
  645.0 9.5 %copy.49 = f32[2,1024,1024]{1,2,0:T(8,128)} copy(f32[2,1024,1024]{1,0,2:T(2,128)} %all-to-all-done) | data formatting | bytes 16777216 | tf_op jit(solution)/shard_map/all_to_all | solution.py:47
  654.5 19.6 %copy.50 = f32[32,2,1024,32]{3,2,1,0:T(8,128)} copy(f32[32,2,1024,32]{2,3,0,1:T(8,128)} %bitcast.155) | data formatting | bytes 16777216 | tf_op jit(solution)/shard_map/all_to_all | solution.py:47
  674.1 20.8 %reshape.284 = f32[64,32768]{1,0:T(8,128)} reshape(f32[32,2,1024,32]{3,2,1,0:T(8,128)} %copy.50) | data formatting | bytes 16777216 | tf_op jit(solution)/shard_map/reshape | solution.py:50
  694.9 13.0 %gather_fusion.1 = f32[64,32768]{1,0:T(8,128)} fusion(f32[64,32768]{1,0:T(8,128)} %reshape.284, s32[1024]{0:T(1024)S(1)} %pad_clamp_fusion), kind=kCustom, calls=%fused_computation.1 | custom fusion | bytes 16777472 | tf_op jit(solution)/shard_map/jit(_take)/gather | solution.py:55
  707.9 12.2 %copy.51 = f32[64,32768]{0,1:T(8,128)} copy(f32[64,32768]{1,0:T(8,128)} %gather_fusion.1) | data formatting | bytes 16777216 | tf_op jit(solution)/shard_map/jit(_take)/gather | solution.py:55
  720.2 11.9 %broadcast_select_fusion = f32[64,1024,32]{0,2,1:T(8,128)} fusion(f32[64,1024,32]{0,2,1:T(8,128)} %bitcast.154, pred[64]{0:T(512)(128)(4,1)S(1)} %compare_and_fusion), kind=kLoop, calls=%fused_computation.10 | loop fusion | flops 2097152 | bytes 16777280 | tf_op jit(solution)/shard_map/jit(_take)/select_n | solution.py:55
  732.0 13.8 %copy.52 = f32[64,1024,32]{1,2,0:T(8,128)} copy(f32[64,1024,32]{0,2,1:T(8,128)} %broadcast_select_fusion) | data formatting | bytes 16777216 | tf_op jit(solution)/shard_map/jit(_take)/select_n | solution.py:55
  745.8 106.2 %all_to_all.33 = f32[64,1024,32]{1,2,0:T(8,128)S(1)} all-to-all(f32[64,1024,32]{1,2,0:T(8,128)} %copy.52), channel_id=1, replica_groups=mesh['row'=32,'col'=4] {'row'}, dimensions={0} | all-to-all | bytes 16777216 | tf_op jit(solution)/shard_map/all_to_all | solution.py:57
  852.1 4.1 copy.53
  856.2 8.7 copy.54
  (126 shorter events, 20.7 us)
Async XLA Ops:
  6.5 541.4 %copy-start = (s32[64]{0:T(128)S(1)}, s32[64]{0:T(128)}, u32[]{:S(2)}) copy-start(s32[64]{0:T(128)} %param.11) | copy-start | bytes 772
  6.5 157.9 %all-gather.2.cloned.1.call-start = ((), (), s32[]{:S(2)}) async-start(), calls=%async_computation.2 | async-start | bytes 20971520 | tf_op jit(solution)/shard_map/all_gather | solution.py:31
  7.3 304.6 %all-reduce.3.cloned.1.call-start = ((), (), s32[]{:S(2)}) async-start(), calls=%async_computation.3 | async-start | bytes 8388608 | tf_op jit(solution)/shard_map/psum | solution.py:21
  198.7 299.2 %all-reduce.5.cloned.1.call-start = ((), (), s32[]{:S(2)}) async-start(), calls=%async_computation.4 | async-start | bytes 8388608 | tf_op jit(solution)/shard_map/psum | solution.py:21
  311.8 6.5 copy-start.4
  331.1 14.4 %slice-start = ((s8[8388608]{0:T(1024)(128)(4,1)}), s8[4194304]{0:T(1024)(128)(4,1)S(1)}, s32[]{:S(2)}) async-start(s8[8388608]{0:T(1024)(128)(4,1)} %bitcast.156), calls=%async_computation.5 | async-start | bytes 8388608
  344.6 2.2 slice-start.1
  346.8 2.2 copy-start.2
  497.9 6.5 copy-start.5
  517.2 4.6 slice-start.2
  520.9 3.5 slice-start.3
  520.9 3.4 copy-start.3
  541.2 103.8 %all-to-all-start = ((f32[2,1024,1024]{1,0,2:T(2,128)}), f32[2,1024,1024]{1,0,2:T(2,128)}, u32[]{:S(2)}, u32[]{:S(2)}) async-start(f32[2,1024,1024]{1,0,2:T(2,128)} %copy.48), calls=%async_computation | async-start | bytes 16777216 | tf_op jit(solution)/shard_map/all_to_all | solution.py:47
  856.2 8.7 copy-start.1
Sparse Core Ops, SparseCore 0:
  9.0 155.3 all-gather.1
  198.8 112.9 all-reduce.2
  385.8 112.0 all-reduce.4
where the time goes:
time: 881 us; the launch traced here: 872 us
  waiting for transfers between devices  260 us (30%)
  other arithmetic  181 us (21%)
  local copies, waits for them, and re-layouts  180 us (20%)
  matrix products  124 us (14%)
  blocking collectives  106 us (12%)
  between operations  14.1 us (2%)
    another operation x5, other arithmetic, unit_solve(): lax.linalg.triangular_solve(lower, right, left_side=True, lower=True, tra...  165 us
    all_gather x1, waiting for transfers between devices, body(): columns = lax.all_gather(panel, 'col', axis=2, tiled=True)  149 us
    all_to_all x1, blocking collectives, body(): lax.all_to_all(returning, 'row', split_axis=0, concat_axis=2, tiled=True)  106 us
    all_to_all x1, waiting for transfers between devices, body(): lax.all_to_all(finished, 'row', split_axis=2, concat_axis=0, tiled=True)  96.3 us
    dot_general x2, matrix products, contract(): jnp.einsum('lic,lir->cr', part, values * weight[:, None, None], precision...  68.4 us
    another operation x30, matrix products, unit_solve(): lax.linalg.triangular_solve(lower, right, left_side=True, lower=True, tra...  55.1 us
    another operation x59, local copies, waits for them, and re-layouts, unit_solve(): lax.linalg.triangular_solve(lower, right, left_side=True, lower=True, tra...  46.5 us
    all_to_all x2, local copies, waits for them, and re-layouts, body(): lax.all_to_all(finished, 'row', split_axis=2, concat_axis=0, tiled=True)  29.1 us
  transfers between devices with their start and end apart: 4, of which 4 were waited for; matrix products, arithmetic and copies ran while one was open for 25% of the time, Pallas kernels for 0%

commit v1 on v0

v1 whole, which is shorter than its diff:
```python
import functools

import jax
import jax.numpy as jnp
from jax import lax
from jax.experimental import pallas as pl
from jax.experimental.pallas import tpu as pltpu
from jax.sharding import PartitionSpec as P

MESH = pl.DeviceIdType.MESH
F32 = jnp.float32
BF16 = jnp.bfloat16
DMA = pltpu.SemaphoreType.DMA

ORDER = (20, 21, 1, 12, 24, 13, 25, 18, 6, 19, 7, 22, 2, 23, 3, 28, 8, 29, 9, 4, 16, 5, 17, 10, 30, 11, 31, 14, 26, 15, 27)


def split(v):
    hi = v.astype(BF16)
    return hi, (v - hi.astype(F32)).astype(BF16)


def dot_high(a, b):
    return jnp.dot(a, b, precision=lax.Precision.HIGHEST, preferred_element_type=F32)


def inverse_unit_lower(low):
    rows = lax.broadcasted_iota(jnp.int32, (128, 128), 0)
    cols = lax.broadcasted_iota(jnp.int32, (128, 128), 1)

    def part(s):
        keep = (rows // (2 * s) == cols // (2 * s)) & ((rows // s) % 2 == 1) & ((cols // s) % 2 == 0)
        return jnp.where(keep, low, 0.0)

    inv = jnp.where(rows == cols, 1.0, 0.0) - part(1)
    for s in (2, 4, 8, 16, 32, 64):
        inv = inv - dot_high(dot_high(inv, part(s)), inv)
    return inv


def main_kernel(
    state, panel, piv, out, z1t, z0t, gath, ufull,
    zst, zhi, zlo, cst, chi, clo, st, xc, bx, bz, cx, cz, first, second, upc, dinv, dblk, rt, sol, rhs, u0,
    ysend, yrecv, asend, arecv, usend, urecv, rsend, rrecv, gsend, grecv, local,
):
    p = lax.axis_index("row")
    y = lax.axis_index("col")
    z, x, c = p // 8, (p // 2) % 4, p % 2

    def row_of(zz, xx, cc):
        return ((zz % 4) * 4 + xx % 4) * 2 + cc

    def peer(k):
        return row_of(z + k // 8, x + (k // 2) % 4, (c + k % 2) % 2)

    sibling = row_of(z, x, 1 - c)

    def rcopy(src, dst, ss, rs, row, col):
        return pltpu.make_async_remote_copy(src, dst, ss, rs, device_id=(row, col), device_id_type=MESH)

    def wait_recv(ref, rs):
        rcopy(ref, ref, rs, rs, sibling, y).wait_recv()

    def wait_send(ref, ss):
        rcopy(ref, ref, ss, ss, sibling, y).wait_send()

    right, left, across = (y + 1) % 4, (y + 3) % 4, (y + 2) % 4

    barrier = pltpu.get_barrier_semaphore()
    for k in range(1, 32):
        pl.semaphore_signal(barrier, inc=1, device_id=(peer(k), y), device_id_type=MESH)
    for d in (right, left, across):
        pl.semaphore_signal(barrier, inc=1, device_id=(p, d), device_id_type=MESH)
    pl.semaphore_wait(barrier, 34)

    y_own = [
        rcopy(panel.at[0], gath.at[3, 0], ysend.at[0], yrecv.at[0], p, right),
        rcopy(panel.at[1], gath.at[1, 1], ysend.at[1], yrecv.at[1], p, left),
        rcopy(panel.at[1], gath.at[3, 1], ysend.at[2], yrecv.at[2], p, right),
        rcopy(panel.at[0], gath.at[1, 0], ysend.at[3], yrecv.at[3], p, left),
    ]
    y_fwd = [
        rcopy(gath.at[3, 0], gath.at[2, 0], ysend.at[4], yrecv.at[4], p, right),
        rcopy(gath.at[1, 1], gath.at[2, 1], ysend.at[5], yrecv.at[5], p, left),
    ]

    lane1 = pl.ds(pl.multiple_of(y * 512, 512), 512)
    lane0 = pl.ds(pl.multiple_of(2048 + (y % 2) * 512, 512), 512)

    def scatter(lanes, sem):
        for k in range(1, 32):
            q = peer(k)
            rows = pl.ds(pl.multiple_of(q * 32, 32), 32)
            rcopy(panel.at[0, rows], upc.at[:, lanes], usend.at[sem], urecv.at[sem], q, y).start()
        rows = pl.ds(pl.multiple_of(p * 32, 32), 32)
        pltpu.make_async_copy(panel.at[0, rows], upc.at[:, lanes], urecv.at[sem]).start()

    def scatter_done(sem):
        wait_send(panel.at[0, pl.ds(0, 31 * 32)], usend.at[sem])

    def u_round_y():
        wait_recv(upc.at[:, pl.ds(0, 512)], urecv.at[0])
        for d in (right, left, across):
            rcopy(upc.at[:, lane1], upc.at[:, lane1], usend.at[2], urecv.at[2], p, d).start()

        @pl.when(y < 2)
        def _():
            wait_recv(upc.at[:, pl.ds(0, 512)], urecv.at[1])
            for d in (right, left, across):
                rcopy(upc.at[:, lane0], upc.at[:, lane0], usend.at[3], urecv.at[3], p, d).start()

    def u_here():
        wait_recv(upc.at[:, pl.ds(0, 1536)], urecv.at[2])

        @pl.when(y < 2)
        def _():
            wait_recv(upc.at[:, pl.ds(0, 512)], urecv.at[3])

        @pl.when(y >= 2)
        def _():
            wait_recv(upc.at[:, pl.ds(0, 1024)], urecv.at[3])

    def gather_a(share, full, h, base):
        pltpu.make_async_copy(share, full.at[z, x, c], local.at[10 + base // 5]).start()
        for d in (1, 3, 2):
            rcopy(share.at[:, pl.ds(0, h)], full.at[z, x, c, :, pl.ds(0, h)], gsend.at[base], grecv.at[base],
                  row_of(z, x + d, c), y).start()
            rcopy(share.at[:, pl.ds(h, h)], full.at[z, x, c, :, pl.ds(h, h)], gsend.at[base + 1], grecv.at[base + 1],
                  row_of(z + d, x, c), y).start()

    def gather_b(share, full, h, base):
        pltpu.make_async_copy(share, full.at[z, x, c], local.at[10 + base // 5]).wait()
        wait_recv(full.at[0, pl.ds(0, 3), 0, :, pl.ds(0, h)], grecv.at[base])
        for d in (1, 3, 2):
            here = full.at[z, :, c, :, pl.ds(0, h)]
            rcopy(here, here, gsend.at[base + 2], grecv.at[base + 2], row_of(z + d, x, c), y).start()
        wait_recv(full.at[0, pl.ds(0, 3), 0, :, pl.ds(0, h)], grecv.at[base + 1])
        for d in (1, 3, 2):
            here = full.at[:, x, c, :, pl.ds(h, h)]
            rcopy(here, here, gsend.at[base + 3], grecv.at[base + 3], row_of(z, x + d, c), y).start()

    def gather_c(full, h, base):
        wait_recv(full.at[pl.ds(0, 3), :, 0, :, pl.ds(0, h)], grecv.at[base + 2])
        wait_recv(full.at[pl.ds(0, 3), :, 0, :, pl.ds(0, h)], grecv.at[base + 3])
        rcopy(full.at[:, :, c], full.at[:, :, c], gsend.at[base + 4], grecv.at[base + 4], sibling, y).start()

    def gather_end(full, base):
        wait_recv(full.at[:, :, 0], grecv.at[base + 4])

    def gather_sent(full, h, base):
        for i in (0, 1):
            wait_send(full.at[0, pl.ds(0, 3), 0, :, pl.ds(0, h)], gsend.at[base + i])
        for i in (2, 3):
            wait_send(full.at[pl.ds(0, 3), :, 0, :, pl.ds(0, h)], gsend.at[base + i])
        wait_send(full.at[:, :, 0], gsend.at[base + 4])

    def first_sends(lo, hi):
        for k in ORDER[lo:hi]:
            q = peer(k)
            rows = pl.ds(pl.multiple_of(q * 32, 32), 32)
            rcopy(state.at[:, rows], first.at[z, x, c], asend.at[0], arecv.at[0], q, y).start()

    my_rows = pl.ds(pl.multiple_of(p * 32, 32), 32)

    def second_sends(lo, hi):
        for k in ORDER[lo:hi]:
            q = peer(k)
            rcopy(second.at[q], out.at[:, my_rows], asend.at[1], arecv.at[1], q, y).start()

    def reorder():
        @pl.loop(0, 32)
        def _(q):
            for slot in range(2):
                b = piv[slot * 32 + q]
                owner = b % 32
                second[q, slot] = first[owner // 8, (owner // 2) % 4, owner % 2, b // 32]

    def transposed(slot, part, buf):
        pltpu.make_async_copy(
            state.at[slot, pl.ds(part * 256, 256)], zst.at[buf], local.at[buf]).wait()

        @pl.loop(0, 4)
        def _(j):
            rows = pl.ds(pl.multiple_of(j * 256, 256), 256)
            hi, lo = split(zst[buf, :, rows].T)
            zhi[slot, rows, part * 256:part * 256 + 256] = hi
            zlo[slot, rows, part * 256:part * 256 + 256] = lo

    def load_state(slot, part, buf):
        pltpu.make_async_copy(
            state.at[slot, pl.ds(part * 256, 256)], zst.at[buf], local.at[buf]).start()

    def load_panel(src, buf):
        pltpu.make_async_copy(src, cst.at[buf], local.at[3 + buf]).start()

    keep = jnp.where(p >= 2, 1.0, 0.0).astype(F32)

    def product(k, slot, buf, new):
        pltpu.make_async_copy(panel.at[0], cst.at[buf], local.at[3 + buf]).wait()
        q = (y + k) % 4
        mark = jnp.where(((p == 0) & (q < 2)) | ((p == 1) & (q >= 2)), -1.0, 0.0).astype(F32)

        @pl.loop(0, 8)
        def _(i):
            rows = pl.ds(pl.multiple_of(i * 128, 128), 128)
            v = cst[buf, rows]
            if slot == 0:
                rr = lax.broadcasted_iota(jnp.int32, (128, 512), 0) + i * 128
                cc = lax.broadcasted_iota(jnp.int32, (128, 512), 1) + (q % 2) * 512
                v = v * keep + jnp.where(rr == cc, mark, 0.0)
            hi, lo = split(v)
            chi[rows] = hi
            clo[rows] = lo

        @pl.loop(0, 4)
        def _(j):
            rows = pl.ds(pl.multiple_of(j * 256, 256), 256)
            a_hi, a_lo = zhi[slot, rows], zlo[slot, rows]
            b_hi = chi[...]
            acc = jnp.dot(a_hi, b_hi, preferred_element_type=F32)
            acc += jnp.dot(a_hi, clo[...], preferred_element_type=F32)
            acc += jnp.dot(a_lo, b_hi, preferred_element_type=F32)
            acc = acc.reshape(4, 2, 32, 512)
            if new:
                st[k, j] = acc
            else:
                st[k, j] = st[k, j] + acc

    def rs_core(k):
        rcopy(st.at[k, :, :, 1 - c], xc.at[k], rsend.at[5 * k], rrecv.at[5 * k], sibling, y).start()

    def rs_one(k):
        wait_recv(xc.at[k], rrecv.at[5 * k])

        @pl.loop(0, 16)
        def _(i):
            xc[k, i // 4, i % 4] = xc[k, i // 4, i % 4] + st[k, i // 4, i % 4, c]

        for d in (1, 3, 2):
            rcopy(xc.at[k, :, (x + d) % 4, :, pl.ds(0, 256)], bx.at[k, d - 1], rsend.at[5 * k + 1],
                  rrecv.at[5 * k + 1], row_of(z, x + d, c), y).start()
            rcopy(xc.at[k, (z + d) % 4, :, :, pl.ds(256, 256)], bz.at[k, d - 1], rsend.at[5 * k + 2],
                  rrecv.at[5 * k + 2], row_of(z + d, x, c), y).start()

    def rs_two(k):
        wait_recv(bx.at[k], rrecv.at[5 * k + 1])
        for i in range(4):
            bx[k, 0, i] = bx[k, 0, i] + bx[k, 1, i] + bx[k, 2, i] + xc[k, i, x, :, 0:256]
        for d in (1, 3, 2):
            rcopy(bx.at[k, 0, (z + d) % 4], cx.at[k, d - 1], rsend.at[5 * k + 3], rrecv.at[5 * k + 3],
                  row_of(z + d, x, c), y).start()
        wait_recv(bz.at[k], rrecv.at[5 * k + 2])
        for i in range(4):
            bz[k, 0, i] = bz[k, 0, i] + bz[k, 1, i] + bz[k, 2, i] + xc[k, z, i, :, 256:512]
        for d in (1, 3, 2):
            rcopy(bz.at[k, 0, (x + d) % 4], cz.at[k, d - 1], rsend.at[5 * k + 4], rrecv.at[5 * k + 4],
                  row_of(z, x + d, c), y).start()

    def rs_three(k):
        q = (y + k) % 4
        wait_recv(cx.at[k], rrecv.at[5 * k + 3])
        rt[q, :, 0:256] = bx[k, 0, z] + cx[k, 0] + cx[k, 1] + cx[k, 2]
        wait_recv(cz.at[k], rrecv.at[5 * k + 4])
        rt[q, :, 256:512] = bz[k, 0, x] + cz[k, 0] + cz[k, 1] + cz[k, 2]

    def rs_sent(k):
        wait_send(xc.at[k], rsend.at[5 * k])
        wait_send(bx.at[k], rsend.at[5 * k + 1])
        wait_send(bz.at[k], rsend.at[5 * k + 2])
        wait_send(cx.at[k], rsend.at[5 * k + 3])
        wait_send(cz.at[k], rsend.at[5 * k + 4])

    def blocks_in():
        for j in range(8):
            rows = (j // 2, pl.ds((j % 2) * 2, 2))
            pltpu.make_async_copy(
                ufull.at[rows[0], rows[1], :, :, pl.ds(1024 + 128 * j, 128)], dblk.at[j], local.at[5]).start()
            pltpu.make_async_copy(
                ufull.at[rows[0], rows[1], :, :, pl.ds(2048 + 128 * j, 128)], dblk.at[8 + j], local.at[5]).start()
        pltpu.make_async_copy(dblk, dblk, local.at[5]).wait()

    def inverses():
        @pl.loop(0, 4)
        def _(g):
            for i in range(4):
                dinv[g * 4 + i] = inverse_unit_lower(dblk[g * 4 + i].reshape(128, 128))

    def u_copies():
        return [
            pltpu.make_async_copy(ufull.at[:, :, :, :, pl.ds(1024, 1024)], first.at[:, :, :, 0], local.at[6]),
            pltpu.make_async_copy(ufull.at[:, :, :, :, pl.ds(0, 1024)], first.at[:, :, :, 1], local.at[7]),
            pltpu.make_async_copy(ufull.at[:, :, :, :, pl.ds(2048, 1024)], u0, local.at[8]),
        ]

    def substitute(base, upper):
        for j in range(7, -1, -1):
            xj = dot_high(rhs[:, 128 * j:128 * j + 128], dinv[base + j])
            sol[base // 8, :, 128 * j:128 * j + 128] = xj
            if j:
                rhs[:, 0:128 * j] = rhs[:, 0:128 * j] - dot_high(xj, upper(j))

    y_own[0].start()
    y_own[1].start()

    @pl.when(p == 1)
    def _():
        scatter(lane1, 0)

    @pl.when((p == 0) & (y < 2))
    def _():
        scatter(lane0, 1)

    pltpu.make_async_copy(state.at[:, my_rows], first.at[z, x, c], local.at[9]).start()
    first_sends(0, 8)

    load_state(0, 0, 0)
    load_panel(panel.at[0], 0)
    load_panel(panel.at[1], 1)
    for t in range(8):
        if t < 7:
            load_state((t + 1) // 4, (t + 1) % 4, (t + 1) % 2)
        transposed(t // 4, t % 4, t % 2)
    product(0, 0, 0, True)
    u_round_y()
    y_own[2].start()
    y_own[3].start()
    first_sends(8, 12)
    product(0, 1, 1, False)
    rs_core(0)
    rs_one(0)
    first_sends(12, 16)

    y_own[0].wait_recv()
    y_fwd[0].start()
    load_panel(gath.at[3, 0], 0)
    y_own[1].wait_recv()
    y_fwd[1].start()
    load_panel(gath.at[1, 1], 1)
    product(3, 0, 0, True)
    u_here()
    gather_a(upc, ufull, 1536, 0)
    first_sends(16, 21)
    product(1, 1, 1, True)
    rs_two(0)
    gather_b(upc, ufull, 1536, 0)
    first_sends(21, 31)
    rs_three(0)

    y_own[2].wait_recv()
    load_panel(gath.at[3, 1], 0)
    y_own[3].wait_recv()
    load_panel(gath.at[1, 0], 1)
    product(3, 1, 0, False)
    rs_core(3)
    product(1, 0, 1, False)
    rs_core(1)
    gather_c(ufull, 1536, 0)
    rs_one(3)
    rs_one(1)
    gather_end(ufull, 0)
    blocks_in()
    inverses()

    pltpu.make_async_copy(state.at[:, my_rows], first.at[z, x, c], local.at[9]).wait()
    wait_recv(second.at[pl.ds(0, 31)], arecv.at[0])
    reorder()
    pltpu.make_async_copy(second.at[p], out.at[:, my_rows], local.at[9]).start()
    second_sends(0, 5)
    rs_two(3)
    rs_two(1)
    uc = u_copies()
    for copy in uc:
        copy.start()

    y_fwd[0].wait_recv()
    load_panel(gath.at[2, 0], 0)
    y_fwd[1].wait_recv()
    load_panel(gath.at[2, 1], 1)
    product(2, 0, 0, True)
    product(2, 1, 1, False)
    rs_core(2)
    second_sends(5, 10)
    rs_one(2)
    second_sends(10, 15)
    rs_three(3)
    rs_three(1)
    rs_two(2)
    second_sends(15, 20)
    rs_three(2)


    def row_block(j, slot, lanes):
        return first[j // 2, (j % 2) * 2:(j % 2) * 2 + 2, :, slot, :, 0:lanes].reshape(128, lanes)

    rhs[:, 0:512] = -rt[2]
    rhs[:, 512:1024] = -rt[3]
    uc[0].wait()
    substitute(0, lambda j: row_block(j, 0, 128 * j))
    gather_a(sol.at[0], z1t, 512, 5)
    second_sends(20, 24)
    rhs[:, 0:512] = -rt[0]
    rhs[:, 512:1024] = -rt[1]
    uc[1].wait()
    for j in range(8):
        rhs[...] = rhs[...] - dot_high(sol[0, :, 128 * j:128 * j + 128], row_block(j, 1, 1024))
    uc[2].wait()
    substitute(8, lambda j: u0[j // 2, (j % 2) * 2:(j % 2) * 2 + 2, :, :, 0:128 * j].reshape(128, 128 * j))
    gather_b(sol.at[0], z1t, 512, 5)
    gather_a(sol.at[1], z0t, 512, 10)
    second_sends(24, 31)
    gather_c(z1t, 512, 5)
    gather_b(sol.at[1], z0t, 512, 10)
    gather_c(z0t, 512, 10)
    gather_end(z1t, 5)
    gather_end(z0t, 10)
    wait_recv(second.at[pl.ds(0, 31)], arecv.at[1])
    pltpu.make_async_copy(second.at[p], out.at[:, my_rows], local.at[9]).wait()

    for d in y_own + y_fwd:
        d.wait_send()

    @pl.when(p == 1)
    def _():
        scatter_done(0)

    @pl.when((p == 0) & (y < 2))
    def _():
        scatter_done(1)

    wait_send(upc.at[:, pl.ds(0, 1536)], usend.at[2])

    @pl.when(y < 2)
    def _():
        wait_send(upc.at[:, pl.ds(0, 1536)], usend.at[3])

    for i in range(2):
        wait_send(second.at[pl.ds(0, 31)], asend.at[i])
    for k in range(4):
        rs_sent(k)
    gather_sent(ufull, 1536, 0)
    gather_sent(z1t, 512, 5)
    gather_sent(z0t, 512, 10)


def main_call(state, panel, pivots):
    any_spec = pl.BlockSpec(memory_space=pl.ANY)
    shape = jax.ShapeDtypeStruct
    outs = [
        shape((2, 1024, 1024), F32), shape((4, 4, 2, 32, 1024), F32), shape((4, 4, 2, 32, 1024), F32),
        shape((4, 2, 1024, 512), F32), shape((4, 4, 2, 32, 3072), F32),
    ]
    vmem = [
        ((2, 256, 1024), F32), ((2, 1024, 1024), BF16), ((2, 1024, 1024), BF16), ((2, 1024, 512), F32),
        ((1024, 512), BF16), ((1024, 512), BF16), ((4, 4, 4, 2, 32, 512), F32), ((4, 4, 4, 32, 512), F32),
        ((4, 3, 4, 32, 256), F32), ((4, 3, 4, 32, 256), F32), ((4, 3, 32, 256), F32), ((4, 3, 32, 256), F32),
        ((4, 4, 2, 2, 32, 1024), F32), ((32, 2, 32, 1024), F32), ((32, 3072), F32), ((16, 128, 128), F32),
        ((16, 2, 2, 32, 128), F32), ((4, 32, 512), F32), ((2, 32, 1024), F32), ((32, 1024), F32),
        ((4, 4, 2, 32, 1024), F32),
    ]
    sems = [6, 6, 2, 2, 4, 4, 20, 20, 15, 15, 13]
    return pl.pallas_call(
        main_kernel,
        out_shape=outs,
        in_specs=[any_spec, any_spec, pl.BlockSpec(memory_space=pltpu.SMEM)],
        out_specs=[any_spec] * 5,
        scratch_shapes=[pltpu.VMEM(*v) for v in vmem] + [DMA((n,)) for n in sems],
        compiler_params=pltpu.CompilerParams(
            collective_id=0, has_side_effects=True, vmem_limit_bytes=60 << 20),
    )(state, panel, pivots)


def select_kernel(ids, moved, z1, z0, out):
    block = ids[pl.program_id(0)]

    @pl.when(block >= 2)
    def _():
        out[0] = moved[0]

    @pl.when(block == 1)
    def _():
        out[0] = z1[...].T

    @pl.when(block == 0)
    def _():
        out[0] = z0[...].T


def select_call(ids, moved, z1, z0):
    tile = 128

    def solved(which):
        return pl.BlockSpec((1024, tile), lambda l, i, ids: (0, jnp.where(ids[l] == which, i, 0)))

    return pl.pallas_call(
        select_kernel,
        out_shape=jax.ShapeDtypeStruct((2, 1024, 1024), F32),
        grid_spec=pltpu.PrefetchScalarGridSpec(
            num_scalar_prefetch=1, grid=(2, 1024 // tile),
            in_specs=[pl.BlockSpec((1, tile, 1024), lambda l, i, ids: (l, i, 0)), solved(1), solved(0)],
            out_specs=pl.BlockSpec((1, tile, 1024), lambda l, i, ids: (l, i, 0))),
    )(ids, moved, z1, z0)


def body(state, panel, pivots):
    ids = lax.dynamic_slice(pivots.reshape(2, 32), (0, lax.axis_index("row")), (2, 1)).reshape(2)
    moved, z1t, z0t, _, _ = main_call(state, panel, pivots)
    return select_call(ids, moved, z1t.reshape(1024, 1024), z0t.reshape(1024, 1024))


def solution(mesh):
    placed = (P(None, "row", "col"), P(None, "row", "col"), P())
    return jax.shard_map(
        body, mesh=mesh, in_specs=placed, out_specs=P(None, "row", "col"), check_vma=False)
```

time: 881 us -> 409 us (0.46)
  the two profiles are of different devices: /device:TPU:97 before, /device:TPU:118 now
where the time goes in v1:
time: 409 us; the launch traced here: 408 us
  Pallas kernels  407 us (100%)
    pallas_call x1, Pallas kernels, main_call(): pl.pallas_call(main_kernel, out_shape=outs, in_specs=[any_spec, any_spec,...  392 us
    pallas_call x1, Pallas kernels, select_call(): pl.pallas_call(select_kernel, out_shape=jax.ShapeDtypeStruct((2, 1024, 10...  15 us

profile of v1, /device:TPU:118, one launch (start us, length us, event | category | flops | bytes accessed | tf_op | source)
XLA Modules:
  0.0 408.0 jit_solution(1628422543394330610)
XLA Ops:
  0.0 0.7 reshape.12
  0.7 0.8 dynamic-slice_reduce_fusion.ids
  1.5 391.5 %shard_map.37 = (f32[2,1024,1024]{2,1,0:T(8,128)}, f32[4,4,2,32,1024]{4,3,2,1,0:T(8,128)}, f32[4,4,2,32,1024]{4,3,2,1,0:T(8,128)}, f32[4,2,1024,512]{3,2,1,0:T(8,128)}, f32[4,4,2,32,3072]{4,3,2,1,0:T(8,128)}) custom-call(f32[2,1024,1024]{2,1,0:T(8,128)} %state.1, f32[2,1024,512]{2,1,0:T(8,128)} %panel.1, s32[64]{0:T(128)} %piv.1), custom_call_target="tpu_custom_call" | custom-call | tf_op jit(solution)/shard_map/pallas_call | solution.py:461
  393.0 15.0 %shard_map.38 = f32[2,1024,1024]{2,1,0:T(8,128)} custom-call(s32[2]{0:T(128)} %dynamic-slice_reduce_fusion.ids, f32[2,1024,1024]{2,1,0:T(8,128)} %get-tuple-element.8.moved, f32[1024,1024]{1,0:T(8,128)} %bitcast.2, f32[1024,1024]{1,0:T(8,128)} %bitcast.3), custom_call_target="tpu_custom_call" | custom-call | tf_op jit(solution)/shard_map/pallas_call | solution.py:494

commit v2 on v1

--- a/solution.py
+++ b/solution.py
@@ -39,8 +39,8 @@
 
 
 def main_kernel(
-    state, panel, piv, out, z1t, z0t, gath, ufull,
-    zst, zhi, zlo, cst, chi, clo, st, xc, bx, bz, cx, cz, first, second, upc, dinv, dblk, rt, sol, rhs, u0,
+    state, panel, piv, out, solved, gath, ufull,
+    zst, zhi, zlo, cst, chi, clo, st, xc, bx, bz, cx, cz, first, second, upc, packed, dinv, dblk, rt, sol, rhs,
     ysend, yrecv, asend, arecv, usend, urecv, rsend, rrecv, gsend, grecv, local,
 ):
     p = lax.axis_index("row")
@@ -73,27 +73,31 @@
         pl.semaphore_signal(barrier, inc=1, device_id=(p, d), device_id_type=MESH)
     pl.semaphore_wait(barrier, 34)
 
+    top, bottom = pl.ds(0, 512), pl.ds(512, 512)
     y_own = [
-        rcopy(panel.at[0], gath.at[3, 0], ysend.at[0], yrecv.at[0], p, right),
-        rcopy(panel.at[1], gath.at[1, 1], ysend.at[1], yrecv.at[1], p, left),
-        rcopy(panel.at[1], gath.at[3, 1], ysend.at[2], yrecv.at[2], p, right),
-        rcopy(panel.at[0], gath.at[1, 0], ysend.at[3], yrecv.at[3], p, left),
+        rcopy(panel.at[0, top], gath.at[3, 0, top], ysend.at[0], yrecv.at[0], p, right),
+        rcopy(panel.at[1, top], gath.at[1, 1, top], ysend.at[1], yrecv.at[1], p, left),
+        rcopy(panel.at[0, bottom], gath.at[3, 0, bottom], ysend.at[2], yrecv.at[2], p, right),
+        rcopy(panel.at[1, bottom], gath.at[1, 1, bottom], ysend.at[3], yrecv.at[3], p, left),
+        rcopy(panel.at[1], gath.at[3, 1], ysend.at[4], yrecv.at[4], p, right),
+        rcopy(panel.at[0], gath.at[1, 0], ysend.at[5], yrecv.at[5], p, left),
     ]
     y_fwd = [
-        rcopy(gath.at[3, 0], gath.at[2, 0], ysend.at[4], yrecv.at[4], p, right),
-        rcopy(gath.at[1, 1], gath.at[2, 1], ysend.at[5], yrecv.at[5], p, left),
+        rcopy(gath.at[3, 0], gath.at[2, 0], ysend.at[6], yrecv.at[6], p, right),
+        rcopy(gath.at[1, 1], gath.at[2, 1], ysend.at[7], yrecv.at[7], p, left),
     ]
 
     lane1 = pl.ds(pl.multiple_of(y * 512, 512), 512)
     lane0 = pl.ds(pl.multiple_of(2048 + (y % 2) * 512, 512), 512)
 
     def scatter(lanes, sem):
-        for k in range(1, 32):
+        def rows_for(q):
+            return pl.ds(pl.multiple_of((q if sem == 0 else 31 - q) * 32, 32), 32)
+
+        for k in ORDER:
             q = peer(k)
-            rows = pl.ds(pl.multiple_of(q * 32, 32), 32)
-            rcopy(panel.at[0, rows], upc.at[:, lanes], usend.at[sem], urecv.at[sem], q, y).start()
-        rows = pl.ds(pl.multiple_of(p * 32, 32), 32)
-        pltpu.make_async_copy(panel.at[0, rows], upc.at[:, lanes], urecv.at[sem]).start()
+            rcopy(panel.at[0, rows_for(q)], upc.at[:, lanes], usend.at[sem], urecv.at[sem], q, y).start()
+        pltpu.make_async_copy(panel.at[0, rows_for(p)], upc.at[:, lanes], urecv.at[sem]).start()
 
     def scatter_done(sem):
         wait_send(panel.at[0, pl.ds(0, 31 * 32)], usend.at[sem])
@@ -120,45 +124,92 @@
         def _():
             wait_recv(upc.at[:, pl.ds(0, 1024)], urecv.at[3])
 
-    def gather_a(share, full, h, base):
+    def u_pack():
+        g = p // 4
+        for t in range(9):
+            lane = jnp.where(t <= g, 1024 + 128 * t, 2048 + 128 * (t - g - 1))
+            packed[:, 128 * t:128 * t + 128] = upc[:, pl.ds(pl.multiple_of(lane, 128), 128)]
+        packed[:, 1152:2176] = upc[:, 0:1024]
+
+    def gather_a(share, full, h, w, base):
         pltpu.make_async_copy(share, full.at[z, x, c], local.at[10 + base // 5]).start()
         for d in (1, 3, 2):
             rcopy(share.at[:, pl.ds(0, h)], full.at[z, x, c, :, pl.ds(0, h)], gsend.at[base], grecv.at[base],
                   row_of(z, x + d, c), y).start()
-            rcopy(share.at[:, pl.ds(h, h)], full.at[z, x, c, :, pl.ds(h, h)], gsend.at[base + 1], grecv.at[base + 1],
-                  row_of(z + d, x, c), y).start()
-
-    def gather_b(share, full, h, base):
+            rcopy(share.at[:, pl.ds(h, w - h)], full.at[z, x, c, :, pl.ds(h, w - h)], gsend.at[base + 1],
+                  grecv.at[base + 1], row_of(z + d, x, c), y).start()
+
+    def gather_b(share, full, h, w, base):
         pltpu.make_async_copy(share, full.at[z, x, c], local.at[10 + base // 5]).wait()
         wait_recv(full.at[0, pl.ds(0, 3), 0, :, pl.ds(0, h)], grecv.at[base])
         for d in (1, 3, 2):
             here = full.at[z, :, c, :, pl.ds(0, h)]
             rcopy(here, here, gsend.at[base + 2], grecv.at[base + 2], row_of(z + d, x, c), y).start()
-        wait_recv(full.at[0, pl.ds(0, 3), 0, :, pl.ds(0, h)], grecv.at[base + 1])
+        wait_recv(full.at[0, pl.ds(0, 3), 0, :, pl.ds(h, w - h)], grecv.at[base + 1])
         for d in (1, 3, 2):
-            here = full.at[:, x, c, :, pl.ds(h, h)]
+            here = full.at[:, x, c, :, pl.ds(h, w - h)]
             rcopy(here, here, gsend.at[base + 3], grecv.at[base + 3], row_of(z, x + d, c), y).start()
 
-    def gather_c(full, h, base):
+    def gather_c(full, h, w, base):
         wait_recv(full.at[pl.ds(0, 3), :, 0, :, pl.ds(0, h)], grecv.at[base + 2])
-        wait_recv(full.at[pl.ds(0, 3), :, 0, :, pl.ds(0, h)], grecv.at[base + 3])
+        wait_recv(full.at[pl.ds(0, 3), :, 0, :, pl.ds(h, w - h)], grecv.at[base + 3])
         rcopy(full.at[:, :, c], full.at[:, :, c], gsend.at[base + 4], grecv.at[base + 4], sibling, y).start()
 
     def gather_end(full, base):
         wait_recv(full.at[:, :, 0], grecv.at[base + 4])
 
-    def gather_sent(full, h, base):
-        for i in (0, 1):
-            wait_send(full.at[0, pl.ds(0, 3), 0, :, pl.ds(0, h)], gsend.at[base + i])
-        for i in (2, 3):
-            wait_send(full.at[pl.ds(0, 3), :, 0, :, pl.ds(0, h)], gsend.at[base + i])
+    def gather_sent(full, h, w, base):
+        wait_send(full.at[0, pl.ds(0, 3), 0, :, pl.ds(0, h)], gsend.at[base])
+        wait_send(full.at[0, pl.ds(0, 3), 0, :, pl.ds(h, w - h)], gsend.at[base + 1])
+        wait_send(full.at[pl.ds(0, 3), :, 0, :, pl.ds(0, h)], gsend.at[base + 2])
+        wait_send(full.at[pl.ds(0, 3), :, 0, :, pl.ds(h, w - h)], gsend.at[base + 3])
         wait_send(full.at[:, :, 0], gsend.at[base + 4])
 
+    def rows_of(q):
+        return pl.ds(pl.multiple_of(q * 32, 32), 32)
+
     def first_sends(lo, hi):
-        for k in ORDER[lo:hi]:
-            q = peer(k)
-            rows = pl.ds(pl.multiple_of(q * 32, 32), 32)
-            rcopy(state.at[:, rows], first.at[z, x, c], asend.at[0], arecv.at[0], q, y).start()
+        @pl.when(p >= 2)
+        def _():
+            for k in ORDER[lo:hi]:
+                q = peer(k)
+                rcopy(state.at[:, rows_of(q)], first.at[z, x, c], asend.at[0], arecv.at[0], q, y).start()
+
+        @pl.when(p < 2)
+        def _():
+            for k in ORDER[lo:hi]:
+                q = peer(k)
+                rcopy(state.at[1, rows_of(q)], first.at[z, x, c, 1], asend.at[0], arecv.at[0], q, y).start()
+
+    def first_own():
+        first[0, 0, 0, 0] = jnp.zeros((32, 1024), F32)
+        first[0, 0, 1, 0] = jnp.zeros((32, 1024), F32)
+
+        @pl.when(p >= 2)
+        def _():
+            pltpu.make_async_copy(state.at[0, rows_of(p)], first.at[z, x, c, 0], local.at[9]).start()
+            pltpu.make_async_copy(state.at[0, rows_of(p)], first.at[z, x, c, 0], local.at[9]).wait()
+
+        pltpu.make_async_copy(state.at[1, rows_of(p)], first.at[z, x, c, 1], local.at[9]).start()
+        pltpu.make_async_copy(state.at[1, rows_of(p)], first.at[z, x, c, 1], local.at[9]).wait()
+
+    def first_here():
+        @pl.when(p >= 2)
+        def _():
+            wait_recv(second.at[pl.ds(0, 30)], arecv.at[0])
+
+        @pl.when(p < 2)
+        def _():
+            wait_recv(state.at[:, pl.ds(0, 976)], arecv.at[0])
+
+    def first_sent():
+        @pl.when(p >= 2)
+        def _():
+            wait_send(second.at[pl.ds(0, 31)], asend.at[0])
+
+        @pl.when(p < 2)
+        def _():
+            wait_send(state.at[0, pl.ds(0, 992)], asend.at[0])
 
     my_rows = pl.ds(pl.multiple_of(p * 32, 32), 32)
 
@@ -178,7 +229,9 @@
     def transposed(slot, part, buf):
         pltpu.make_async_copy(
             state.at[slot, pl.ds(part * 256, 256)], zst.at[buf], local.at[buf]).wait()
-
+        transposed_body(slot, part, buf)
+
+    def transposed_body(slot, part, buf):
         @pl.loop(0, 4)
         def _(j):
             rows = pl.ds(pl.multiple_of(j * 256, 256), 256)
@@ -197,6 +250,9 @@
 
     def product(k, slot, buf, new):
         pltpu.make_async_copy(panel.at[0], cst.at[buf], local.at[3 + buf]).wait()
+        product_body(k, slot, buf, new)
+
+    def product_body(k, slot, buf, new):
         q = (y + k) % 4
         mark = jnp.where(((p == 0) & (q < 2)) | ((p == 1) & (q >= 2)), -1.0, 0.0).astype(F32)
 
@@ -272,33 +328,59 @@
 
     def blocks_in():
         for j in range(8):
-            rows = (j // 2, pl.ds((j % 2) * 2, 2))
+            lanes = pl.ds(128 * j, 128)
             pltpu.make_async_copy(
-                ufull.at[rows[0], rows[1], :, :, pl.ds(1024 + 128 * j, 128)], dblk.at[j], local.at[5]).start()
-            pltpu.make_async_copy(
-                ufull.at[rows[0], rows[1], :, :, pl.ds(2048 + 128 * j, 128)], dblk.at[8 + j], local.at[5]).start()
+                ufull.at[j // 2, pl.ds((j % 2) * 2, 2), :, :, lanes], dblk.at[j], local.at[5]).start()
+            for i in range(4):
+                m = 31 - 4 * j - i
+                pltpu.make_async_copy(
+                    ufull.at[m // 8, (m // 2) % 4, m % 2, :, pl.ds(1024, 128)], dblk.at[8 + j, i // 2, i % 2],
+                    local.at[5]).start()
         pltpu.make_async_copy(dblk, dblk, local.at[5]).wait()
 
-    def inverses():
-        @pl.loop(0, 4)
+    def inverses(lo, hi):
+        @pl.loop(lo, hi)
         def _(g):
             for i in range(4):
                 dinv[g * 4 + i] = inverse_unit_lower(dblk[g * 4 + i].reshape(128, 128))
 
-    def u_copies():
-        return [
-            pltpu.make_async_copy(ufull.at[:, :, :, :, pl.ds(1024, 1024)], first.at[:, :, :, 0], local.at[6]),
-            pltpu.make_async_copy(ufull.at[:, :, :, :, pl.ds(0, 1024)], first.at[:, :, :, 1], local.at[7]),
-            pltpu.make_async_copy(ufull.at[:, :, :, :, pl.ds(2048, 1024)], u0, local.at[8]),
-        ]
-
-    def substitute(base, upper):
+    u_copies = [
+        pltpu.make_async_copy(ufull.at[:, :, :, :, pl.ds(0, 1024)], first.at[:, :, :, 0], local.at[6]),
+        pltpu.make_async_copy(ufull.at[:, :, :, :, pl.ds(1152, 1024)], first.at[:, :, :, 1], local.at[7]),
+    ]
+
+    def row_block(j, slot, lanes):
+        return first[j // 2, (j % 2) * 2:(j % 2) * 2 + 2, :, slot, :, 0:lanes].reshape(128, lanes)
+
+    def row_block_zero(j):
+        parts = []
+        for i in range(4):
+            m = 31 - 4 * j - i
+            parts.append(first[m // 8, (m // 2) % 4, m % 2, 0, :, 128 * (8 - j):1024])
+        return jnp.concatenate(parts, axis=0)
+
+    def substitute(which, upper):
         for j in range(7, -1, -1):
-            xj = dot_high(rhs[:, 128 * j:128 * j + 128], dinv[base + j])
-            sol[base // 8, :, 128 * j:128 * j + 128] = xj
+            xj = dot_high(rhs[:, 128 * j:128 * j + 128], dinv[8 * which + j])
+            sol[:, 1024 * which + 128 * j:1024 * which + 128 * j + 128] = xj
             if j:
                 rhs[:, 0:128 * j] = rhs[:, 0:128 * j] - dot_high(xj, upper(j))
 
+    def substitute_one():
+        rhs[:, 0:512] = -rt[2]
+        rhs[:, 512:1024] = -rt[3]
+        u_copies[0].wait()
+        substitute(0, lambda j: row_block(j, 0, 128 * j))
+
+    def substitute_zero():
+        rhs[:, 0:512] = -rt[0]
+        rhs[:, 512:1024] = -rt[1]
+        u_copies[1].wait()
+        for j in range(8):
+            rhs[...] = rhs[...] - dot_high(sol[:, 128 * j:128 * j + 128], row_block(j, 1, 1024))
+        substitute(1, row_block_zero)
+
+    U, Z = (1152, 2176, 0), (1024, 2048, 5)
     y_own[0].start()
     y_own[1].start()
 
@@ -310,8 +392,7 @@
     def _():
         scatter(lane0, 1)
 
-    pltpu.make_async_copy(state.at[:, my_rows], first.at[z, x, c], local.at[9]).start()
-    first_sends(0, 8)
+    first_sends(0, 6)
 
     load_state(0, 0, 0)
     load_panel(panel.at[0], 0)
@@ -320,57 +401,62 @@
         if t < 7:
             load_state((t + 1) // 4, (t + 1) % 4, (t + 1) % 2)
         transposed(t // 4, t % 4, t % 2)
+    u_round_y()
+    for i in (2, 3, 4, 5):
+        y_own[i].start()
+    first_sends(6, 10)
+    first_own()
     product(0, 0, 0, True)
-    u_round_y()
-    y_own[2].start()
-    y_own[3].start()
-    first_sends(8, 12)
     product(0, 1, 1, False)
     rs_core(0)
+    u_here()
+    u_pack()
+    gather_a(packed, ufull, *U)
     rs_one(0)
-    first_sends(12, 16)
+    first_sends(10, 15)
+    gather_b(packed, ufull, *U)
+    rs_two(0)
+    first_sends(15, 21)
 
     y_own[0].wait_recv()
+    y_own[2].wait_recv()
     y_fwd[0].start()
     load_panel(gath.at[3, 0], 0)
     y_own[1].wait_recv()
+    y_own[3].wait_recv()
     y_fwd[1].start()
     load_panel(gath.at[1, 1], 1)
     product(3, 0, 0, True)
-    u_here()
-    gather_a(upc, ufull, 1536, 0)
-    first_sends(16, 21)
     product(1, 1, 1, True)
-    rs_two(0)
-    gather_b(upc, ufull, 1536, 0)
-    first_sends(21, 31)
     rs_three(0)
-
-    y_own[2].wait_recv()
+    first_sends(21, 26)
+    gather_c(ufull, *U)
+    first_sends(26, 31)
+
+    y_own[4].wait_recv()
     load_panel(gath.at[3, 1], 0)
-    y_own[3].wait_recv()
+    y_own[5].wait_recv()
     load_panel(gath.at[1, 0], 1)
     product(3, 1, 0, False)
     rs_core(3)
     product(1, 0, 1, False)
     rs_core(1)
-    gather_c(ufull, 1536, 0)
+    gather_end(ufull, 0)
+    blocks_in()
     rs_one(3)
     rs_one(1)
-    gather_end(ufull, 0)
-    blocks_in()
-    inverses()
-
-    pltpu.make_async_copy(state.at[:, my_rows], first.at[z, x, c], local.at[9]).wait()
-    wait_recv(second.at[pl.ds(0, 31)], arecv.at[0])
+    inverses(0, 2)
+    rs_two(3)
+    rs_two(1)
+    first_here()
     reorder()
+    for copy in u_copies:
+        copy.start()
     pltpu.make_async_copy(second.at[p], out.at[:, my_rows], local.at[9]).start()
     second_sends(0, 5)
-    rs_two(3)
-    rs_two(1)
-    uc = u_copies()
-    for copy in uc:
-        copy.start()
+    inverses(2, 4)
+    rs_three(3)
+    rs_three(1)
 
     y_fwd[0].wait_recv()
     load_panel(gath.at[2, 0], 0)
@@ -379,40 +465,20 @@
     product(2, 0, 0, True)
     product(2, 1, 1, False)
     rs_core(2)
-    second_sends(5, 10)
+    second_sends(5, 9)
     rs_one(2)
-    second_sends(10, 15)
-    rs_three(3)
-    rs_three(1)
+    second_sends(9, 13)
     rs_two(2)
-    second_sends(15, 20)
+    second_sends(13, 17)
     rs_three(2)
-
-
-    def row_block(j, slot, lanes):
-        return first[j // 2, (j % 2) * 2:(j % 2) * 2 + 2, :, slot, :, 0:lanes].reshape(128, lanes)
-
-    rhs[:, 0:512] = -rt[2]
-    rhs[:, 512:1024] = -rt[3]
-    uc[0].wait()
-    substitute(0, lambda j: row_block(j, 0, 128 * j))
-    gather_a(sol.at[0], z1t, 512, 5)
-    second_sends(20, 24)
-    rhs[:, 0:512] = -rt[0]
-    rhs[:, 512:1024] = -rt[1]
-    uc[1].wait()
-    for j in range(8):
-        rhs[...] = rhs[...] - dot_high(sol[0, :, 128 * j:128 * j + 128], row_block(j, 1, 1024))
-    uc[2].wait()
-    substitute(8, lambda j: u0[j // 2, (j % 2) * 2:(j % 2) * 2 + 2, :, :, 0:128 * j].reshape(128, 128 * j))
-    gather_b(sol.at[0], z1t, 512, 5)
-    gather_a(sol.at[1], z0t, 512, 10)
-    second_sends(24, 31)
-    gather_c(z1t, 512, 5)
-    gather_b(sol.at[1], z0t, 512, 10)
-    gather_c(z0t, 512, 10)
-    gather_end(z1t, 5)
-    gather_end(z0t, 10)
+    substitute_one()
+    substitute_zero()
+    gather_a(sol, solved, *Z)
+    second_sends(17, 22)
+    gather_b(sol, solved, *Z)
+    second_sends(22, 31)
+    gather_c(solved, *Z)
+    gather_end(solved, 5)
     wait_recv(second.at[pl.ds(0, 31)], arecv.at[1])
     pltpu.make_async_copy(second.at[p], out.at[:, my_rows], local.at[9]).wait()
 
@@ -433,43 +499,42 @@
     def _():
         wait_send(upc.at[:, pl.ds(0, 1536)], usend.at[3])
 
-    for i in range(2):
-        wait_send(second.at[pl.ds(0, 31)], asend.at[i])
+    first_sent()
+    wait_send(second.at[pl.ds(0, 31)], asend.at[1])
     for k in range(4):
         rs_sent(k)
-    gather_sent(ufull, 1536, 0)
-    gather_sent(z1t, 512, 5)
-    gather_sent(z0t, 512, 10)
+    gather_sent(ufull, *U)
+    gather_sent(solved, *Z)
 
 
 def main_call(state, panel, pivots):
     any_spec = pl.BlockSpec(memory_space=pl.ANY)
     shape = jax.ShapeDtypeStruct
     outs = [
-        shape((2, 1024, 1024), F32), shape((4, 4, 2, 32, 1024), F32), shape((4, 4, 2, 32, 1024), F32),
-        shape((4, 2, 1024, 512), F32), shape((4, 4, 2, 32, 3072), F32),
+        shape((2, 1024, 1024), F32), shape((4, 4, 2, 32, 2048), F32),
+        shape((4, 2, 1024, 512), F32), shape((4, 4, 2, 32, 2176), F32),
     ]
     vmem = [
         ((2, 256, 1024), F32), ((2, 1024, 1024), BF16), ((2, 1024, 1024), BF16), ((2, 1024, 512), F32),
         ((1024, 512), BF16), ((1024, 512), BF16), ((4, 4, 4, 2, 32, 512), F32), ((4, 4, 4, 32, 512), F32),
         ((4, 3, 4, 32, 256), F32), ((4, 3, 4, 32, 256), F32), ((4, 3, 32, 256), F32), ((4, 3, 32, 256), F32),
-        ((4, 4, 2, 2, 32, 1024), F32), ((32, 2, 32, 1024), F32), ((32, 3072), F32), ((16, 128, 128), F32),
-        ((16, 2, 2, 32, 128), F32), ((4, 32, 512), F32), ((2, 32, 1024), F32), ((32, 1024), F32),
-        ((4, 4, 2, 32, 1024), F32),
+        ((4, 4, 2, 2, 32, 1024), F32), ((32, 2, 32, 1024), F32), ((32, 3072), F32), ((32, 2176), F32),
+        ((16, 128, 128), F32),
+        ((16, 2, 2, 32, 128), F32), ((4, 32, 512), F32), ((32, 2048), F32), ((32, 1024), F32),
     ]
-    sems = [6, 6, 2, 2, 4, 4, 20, 20, 15, 15, 13]
+    sems = [8, 8, 2, 2, 4, 4, 20, 20, 10, 10, 12]
     return pl.pallas_call(
         main_kernel,
         out_shape=outs,
         in_specs=[any_spec, any_spec, pl.BlockSpec(memory_space=pltpu.SMEM)],
-        out_specs=[any_spec] * 5,
+        out_specs=[any_spec] * 4,
         scratch_shapes=[pltpu.VMEM(*v) for v in vmem] + [DMA((n,)) for n in sems],
         compiler_params=pltpu.CompilerParams(
             collective_id=0, has_side_effects=True, vmem_limit_bytes=60 << 20),
     )(state, panel, pivots)
 
 
-def select_kernel(ids, moved, z1, z0, out):
+def select_kernel(ids, moved, one, zero, out):
     block = ids[pl.program_id(0)]
 
     @pl.when(block >= 2)
@@ -478,33 +543,35 @@
 
     @pl.when(block == 1)
     def _():
-        out[0] = z1[...].T
+        out[0] = one[...].T
 
     @pl.when(block == 0)
     def _():
-        out[0] = z0[...].T
-
-
-def select_call(ids, moved, z1, z0):
-    tile = 128
-
-    def solved(which):
-        return pl.BlockSpec((1024, tile), lambda l, i, ids: (0, jnp.where(ids[l] == which, i, 0)))
+        out[0] = zero[...].T
+
+
+def select_call(ids, moved, solved):
+    tile = 256
+    tiles = 1024 // tile
+
+    def rows_of(which):
+        return pl.BlockSpec(
+            (1024, tile), lambda l, i, ids: (0, (1 - which) * tiles + jnp.where(ids[l] == which, i, 0)))
 
     return pl.pallas_call(
         select_kernel,
         out_shape=jax.ShapeDtypeStruct((2, 1024, 1024), F32),
         grid_spec=pltpu.PrefetchScalarGridSpec(
-            num_scalar_prefetch=1, grid=(2, 1024 // tile),
-            in_specs=[pl.BlockSpec((1, tile, 1024), lambda l, i, ids: (l, i, 0)), solved(1), solved(0)],
+            num_scalar_prefetch=1, grid=(2, tiles),
+            in_specs=[pl.BlockSpec((1, tile, 1024), lambda l, i, ids: (l, i, 0)), rows_of(1), rows_of(0)],
             out_specs=pl.BlockSpec((1, tile, 1024), lambda l, i, ids: (l, i, 0))),
-    )(ids, moved, z1, z0)
+    )(ids, moved, solved, solved)
 
 
 def body(state, panel, pivots):
     ids = lax.dynamic_slice(pivots.reshape(2, 32), (0, lax.axis_index("row")), (2, 1)).reshape(2)
-    moved, z1t, z0t, _, _ = main_call(state, panel, pivots)
-    return select_call(ids, moved, z1t.reshape(1024, 1024), z0t.reshape(1024, 1024))
+    moved, solved, _, _ = main_call(state, panel, pivots)
+    return select_call(ids, moved, solved.reshape(1024, 2048))
 
 
 def solution(mesh):

time: 409 us -> 350 us (0.86)
  the two profiles are of different devices: /device:TPU:118 before, /device:TPU:97 now
where the time goes in v2:
time: 350 us; the launch traced here: 349 us
  Pallas kernels  348 us (99%)
    pallas_call x1, Pallas kernels, main_call(): pl.pallas_call(main_kernel, out_shape=outs, in_specs=[any_spec, any_spec,...  335 us
    pallas_call x1, Pallas kernels, select_call(): pl.pallas_call(select_kernel, out_shape=jax.ShapeDtypeStruct((2, 1024, 10...  12.7 us

profile of v2, /device:TPU:97, one launch (start us, length us, event | category | flops | bytes accessed | tf_op | source)
XLA Modules:
  0.0 349.4 jit_solution(6214172663721548167)
XLA Ops:
  0.0 0.7 reshape.9
  0.7 0.7 dynamic-slice_reduce_fusion.ids
  1.5 335.2 %shard_map.37 = (f32[2,1024,1024]{2,1,0:T(8,128)}, f32[4,4,2,32,2048]{4,3,2,1,0:T(8,128)}, f32[4,2,1024,512]{3,2,1,0:T(8,128)}, f32[4,4,2,32,2176]{4,3,2,1,0:T(8,128)}) custom-call(f32[2,1024,1024]{2,1,0:T(8,128)} %state.1, f32[2,1024,512]{2,1,0:T(8,128)} %panel.1, s32[64]{0:T(128)} %piv.1), custom_call_target="tpu_custom_call" | custom-call | tf_op jit(solution)/shard_map/pallas_call | solution.py:526
  336.7 12.7 %shard_map.38 = f32[2,1024,1024]{2,1,0:T(8,128)} custom-call(s32[2]{0:T(128)} %dynamic-slice_reduce_fusion.ids, f32[2,1024,1024]{2,1,0:T(8,128)} %get-tuple-element.7.moved, f32[1024,2048]{1,0:T(8,128)} %bitcast.1, f32[1024,2048]{1,0:T(8,128)} %bitcast.2), custom_call_target="tpu_custom_call" | custom-call | tf_op jit(solution)/shard_map/pallas_call | solution.py:561

commit v3 on v2

--- a/solution.py
+++ b/solution.py
@@ -534,38 +534,34 @@
     )(state, panel, pivots)
 
 
-def select_kernel(ids, moved, one, zero, out):
+def select_kernel(ids, moved, solved, out):
     block = ids[pl.program_id(0)]
 
     @pl.when(block >= 2)
     def _():
         out[0] = moved[0]
 
-    @pl.when(block == 1)
-    def _():
-        out[0] = one[...].T
-
-    @pl.when(block == 0)
-    def _():
-        out[0] = zero[...].T
+    @pl.when(block < 2)
+    def _():
+        out[0] = solved[...].T
 
 
 def select_call(ids, moved, solved):
     tile = 256
     tiles = 1024 // tile
 
-    def rows_of(which):
-        return pl.BlockSpec(
-            (1024, tile), lambda l, i, ids: (0, (1 - which) * tiles + jnp.where(ids[l] == which, i, 0)))
+    def solved_tile(l, i, ids):
+        return 0, jnp.where(ids[l] < 2, (1 - ids[l]) * tiles + i, 0)
 
     return pl.pallas_call(
         select_kernel,
         out_shape=jax.ShapeDtypeStruct((2, 1024, 1024), F32),
         grid_spec=pltpu.PrefetchScalarGridSpec(
             num_scalar_prefetch=1, grid=(2, tiles),
-            in_specs=[pl.BlockSpec((1, tile, 1024), lambda l, i, ids: (l, i, 0)), rows_of(1), rows_of(0)],
+            in_specs=[pl.BlockSpec((1, tile, 1024), lambda l, i, ids: (l, i, 0)),
+                      pl.BlockSpec((1024, tile), solved_tile)],
             out_specs=pl.BlockSpec((1, tile, 1024), lambda l, i, ids: (l, i, 0))),
-    )(ids, moved, solved, solved)
+    )(ids, moved, solved)
 
 
 def body(state, panel, pivots):

time: 350 us -> 349 us (level)
  no operation moved by 1% of the time
where the time goes in v3:
time: 349 us; the launch traced here: 347 us
  Pallas kernels  345 us (99%)
    pallas_call x1, Pallas kernels, main_call(): pl.pallas_call(main_kernel, out_shape=outs, in_specs=[any_spec, any_spec,...  335 us
    pallas_call x1, Pallas kernels, select_call(): pl.pallas_call(select_kernel, out_shape=jax.ShapeDtypeStruct((2, 1024, 10...  9.98 us

profile of v3, /device:TPU:97, one launch (start us, length us, event | category | flops | bytes accessed | tf_op | source)
XLA Modules:
  0.0 346.7 jit_solution(11604927723580481923)
XLA Ops:
  0.0 0.7 reshape.9
  0.7 0.7 dynamic-slice_reduce_fusion.ids
  1.5 335.2 %shard_map.37 = (f32[2,1024,1024]{2,1,0:T(8,128)}, f32[4,4,2,32,2048]{4,3,2,1,0:T(8,128)}, f32[4,2,1024,512]{3,2,1,0:T(8,128)}, f32[4,4,2,32,2176]{4,3,2,1,0:T(8,128)}) custom-call(f32[2,1024,1024]{2,1,0:T(8,128)} %state.1, f32[2,1024,512]{2,1,0:T(8,128)} %panel.1, s32[64]{0:T(128)} %piv.1), custom_call_target="tpu_custom_call" | custom-call | tf_op jit(solution)/shard_map/pallas_call | solution.py:526
  336.7 10.0 %shard_map.38 = f32[2,1024,1024]{2,1,0:T(8,128)} custom-call(s32[2]{0:T(128)} %dynamic-slice_reduce_fusion.ids, f32[2,1024,1024]{2,1,0:T(8,128)} %get-tuple-element.7.moved, f32[1024,2048]{1,0:T(8,128)} %bitcast.1), custom_call_target="tpu_custom_call" | custom-call | tf_op jit(solution)/shard_map/pallas_call | solution.py:556
